TPU v7x, 512 devices: a whole 4x4x16 slice. The times are simulated.
512 devices in a mesh: sub: 16 (over z), row: 4 (over y), col: 8 (over x, core).
Axes of the slice: x: 4, y: 4, z: 16, core: 2. Of those that a mesh axis runs over, the one named last changes fastest.
Arguments:
- child_factor: float32 [16, 256, 2048], P('sub', None, 'row'), may hold values from -6 to 6
- child_map: int32 [16, 2048], P('sub'), may hold values from 0 to 8191, as said below
- child_len: int32 [16], P('sub'), may hold values from 1 to 2048, 16384 in all
- class_ids: int32 [8192], replicated, may hold values from 0 to 7
- class_kappa: float32 [8], replicated, may hold values from 0.25 to 16
- landmarks: int32 [256], replicated, may hold values from 0 to 1023
- diag_inverse: float32 [2, 512, 512], replicated, as said below
Outputs:
- panel_factor: float32 [2, 512, 16, 512], P(None, 'col', 'sub', 'row')
- landmark_solution: float32 [256, 16, 512], P('col', 'sub', 'row')
Inputs may be any that keep to these rules, and one draw needn't show every extreme that they name: `child_map`: node i of a child maps to parent row 512 a + 128 (i // 512) + u for some block a and some u below 128; the nodes of one child map to distinct rows. `diag_inverse`: each 512 x 512 block is lower triangular with a positive diagonal.
All inputs are finite; a program needn't handle non-finite values. No bound on the sum of `child_len` on one device may be relied on, other than what follows from the above.
Results may differ from a plain program's by a relative error of at most 0.0003.
Values sent between devices are 32-bit elements; how exact they have to be, the bound alone decides.
A program may use at most 64 MiB of HBM per device.

v0:
```python
import jax
import jax.numpy as jnp
from jax import lax
from jax.sharding import PartitionSpec as P

PRECISE = lax.Precision.HIGHEST


def from_root(value, axis, root):
    mine = lax.axis_index(axis) == root
    return lax.psum(jnp.where(mine, value, jnp.zeros_like(value)), axis)


def contract(left_part, right_part, left_dim, right_dim):
    return lax.dot_general(
        left_part,
        right_part,
        (((left_dim,), (right_dim,)), ((), ())),
        precision=PRECISE,
        preferred_element_type=jnp.float32,
    )


def on_device(child_factor, child_map, child_len, class_ids, class_kappa, landmarks, diag_inverse):
    sub_index = lax.axis_index("sub")
    row_index = lax.axis_index("row")
    col_index = lax.axis_index("col")
    sub_count = lax.axis_size("sub")
    row_count = lax.axis_size("row")
    col_count = lax.axis_size("col")
    panels = diag_inverse.shape[0]
    width_panel = diag_inverse.shape[1]
    total_nodes = class_ids.shape[0]
    col_width = width_panel // col_count
    quarter = width_panel // row_count
    quarter_rows = total_nodes // row_count
    local_rows = quarter_rows // sub_count
    blocks_local = local_rows // quarter
    node_quarter = child_factor.shape[2]
    own_cols = (
        jnp.arange(panels, dtype=jnp.int32)[:, None] * width_panel
        + col_index * col_width
        + jnp.arange(col_width, dtype=jnp.int32)[None, :]
    ).reshape(-1)
    node_map = child_map[0]
    node_index = row_index * node_quarter + jnp.arange(node_quarter, dtype=jnp.int32)
    live_factor = jnp.where((node_index < child_len[0])[None, :], child_factor[0], jnp.float32(0.0))
    select = (node_map[:, None] == own_cols[None, :]).astype(jnp.float32)
    reduced = jnp.dot(
        lax.all_gather(live_factor, "row", axis=1, tiled=True), select, precision=PRECISE
    )
    partial_cols = jnp.zeros((node_quarter, own_cols.shape[0]), jnp.float32) - contract(
        live_factor, reduced, 0, 0
    )
    parent = lax.dynamic_slice_in_dim(node_map, row_index * node_quarter, node_quarter)
    target = parent // width_panel * quarter + parent % width_panel - row_index * quarter
    place_rows = (target[:, None] == jnp.arange(quarter_rows, dtype=jnp.int32)[None, :]).astype(
        jnp.float32
    )
    contribution = contract(partial_cols, place_rows, 0, 0)
    front_cols = lax.psum_scatter(contribution, "sub", scatter_dimension=1, tiled=True)
    class_table = (
        class_ids[:, None] == jnp.arange(class_kappa.shape[0], dtype=jnp.int32)[None, :]
    ).astype(jnp.float32)
    coefficient = jnp.sum(class_table * class_kappa[None, :], axis=1) + jnp.float32(4.0)
    local_index = jnp.arange(local_rows, dtype=jnp.int32)
    global_rows = (
        (sub_index * blocks_local + local_index // quarter) * width_panel
        + row_index * quarter
        + local_index % quarter
    )
    coeff_row = jnp.take(coefficient, global_rows)[None, :]
    coeff_col = jnp.take(coefficient, own_cols)[:, None]
    offset_band = global_rows[None, :] - own_cols[:, None]
    end_count = jnp.where(
        (global_rows == 0) | (global_rows == total_nodes - 1), jnp.float32(1.0), jnp.float32(2.0)
    )[None, :]
    band_part = jnp.where(
        offset_band == 0,
        coeff_row * coeff_row + end_count,
        jnp.where(
            jnp.abs(offset_band) == 1,
            -(coeff_row + coeff_col),
            jnp.where(jnp.abs(offset_band) == 2, jnp.float32(1.0), jnp.float32(0.0)),
        ),
    )
    front_cols = front_cols + band_part
    land_count = landmarks.shape[0] // col_count
    chooser = (landmarks[:, None] == own_cols[None, :]).astype(jnp.float32)
    right_side = lax.psum_scatter(
        jnp.dot(chooser, front_cols, precision=PRECISE), "col", scatter_dimension=0, tiled=True
    )
    column_slabs = [slab for slab in front_cols.reshape(panels, col_width, local_rows)]
    inner_index = jnp.arange(width_panel, dtype=jnp.int32)
    block_of_row = global_rows // width_panel
    pieces = []
    for panel_index in range(panels):
        inverse = diag_inverse[panel_index]
        panel_now = contract(
            lax.all_gather(column_slabs[panel_index], "col", axis=0, tiled=True), inverse, 0, 1
        )
        keep_mask = global_rows[:, None] - panel_index * width_panel >= inner_index[None, :]
        panel_now = jnp.where(keep_mask, panel_now, jnp.float32(0.0))
        pieces.append(lax.dynamic_slice_in_dim(panel_now, col_index * col_width, col_width, 1).T)
        for later_panel in range(panel_index + 1, panels):
            owner_sub = later_panel // blocks_local
            whole_block = from_root(
                lax.all_gather(panel_now, "row", axis=0, tiled=True), "sub", owner_sub
            )
            my_slice = lax.dynamic_slice_in_dim(whole_block, col_index * col_width, col_width, 0)
            column_slabs[later_panel] = column_slabs[later_panel] - contract(
                my_slice, panel_now, 1, 1
            )
        owner_sub = panel_index // blocks_local
        gathered = lax.all_gather(right_side, "row", axis=1, tiled=True)
        values = from_root(contract(gathered, inverse, 1, 1), "sub", owner_sub)
        below_update = contract(values, panel_now, 1, 1)
        settled = jnp.tile(
            lax.dynamic_slice_in_dim(values, row_index * quarter, quarter, 1), (1, blocks_local)
        )
        right_side = jnp.where(
            (block_of_row > panel_index)[None, :],
            right_side - below_update,
            jnp.where((block_of_row == panel_index)[None, :], settled, right_side),
        )
    panel_factor = jnp.stack(pieces).reshape(panels, col_width, blocks_local, quarter)
    landmark_solution = right_side.reshape(land_count, blocks_local, quarter)
    return (panel_factor, landmark_solution)


def solution(mesh):
    return jax.shard_map(
        on_device,
        mesh=mesh,
        in_specs=(P("sub", None, "row"), P("sub", None), P("sub"), P(), P(), P(), P()),
        out_specs=(P(None, "col", "sub", "row"), P("col", "sub", "row")),
        check_vma=False,
    )
```

profile of v0, /device:TPU:1, one launch (start us, length us, event | category | flops | bytes accessed | tf_op | source)
XLA Modules:
  0.0 513.7 jit_solution(16760685932046861145)
XLA Ops:
  7.2 0.0 all-gather.3.cloned.1.call-start
  7.9 1.9 bitcast_select_fusion
  9.8 0.0 all-gather.3.cloned.1.call-update
  9.8 0.0 reduce-scatter.3.cloned.1.call-start
  9.9 0.1 iota_add_fusion
  9.9 0.1 add.292
  10.0 0.7 constant_dynamic-slice_fusion
  10.7 43.3 %all-gather.3.cloned.1.call-done = f32[256,2048]{1,0:T(8,128)} async-done(((f32[256,512]{1,0:T(8,128)}), f32[256,2048]{1,0:T(8,128)}) %all-gather.3.cloned.1.call-update) | async-done | bytes 2097168 | tf_op jit(solution)/shard_map/all_gather | solution.py:50
  54.0 2.8 fusion.8
  56.8 0.0 copy-start.5
  56.8 0.0 copy-start.7
  56.8 1.0 convolution_subtract_fusion
  57.8 0.0 copy-start.6
  57.9 2.7 fusion
  60.5 0.0 reduce-scatter.3.cloned.1.call-update
  60.5 0.0 reduce-scatter.5.cloned.1.call-start
  60.7 0.1 select_reduce_fusion
  60.8 1.1 gather_fusion
  62.0 1.1 gather_fusion.1
  63.2 58.0 %reduce-scatter.3.cloned.1.call-done = f32[128,128]{1,0:T(8,128)} async-done(((f32[128,2048]{1,0:T(8,128)}), f32[128,128]{1,0:T(8,128)}) %reduce-scatter.3.cloned.1.call-update) | async-done | bytes 65552 | tf_op jit(solution)/shard_map/reduce_scatter | solution.py:61
  121.2 0.9 select_add_fusion
  122.2 0.9 fusion.17
  123.1 0.0 reduce-scatter.5.cloned.1.call-update
  123.1 0.0 all-reduce.4.cloned.1.call-start
  123.2 23.6 %all_gather.19 = f32[512,128]{1,0:T(8,128)S(1)} all-gather(f32[64,128]{1,0:T(8,128)S(1)} %unstack.10), channel_id=1, replica_groups=mesh['sub'=16,'row'=4,'col'=8] {'col'}, dimensions={0}, use_global_device_ids=true | all-gather | bytes 294912 | tf_op jit(solution)/shard_map/all_gather | solution.py:100
  146.8 21.6 %reduce-scatter.5.cloned.1.call-done = f32[32,128]{1,0:T(8,128)} async-done(((f32[256,128]{1,0:T(8,128)}), f32[32,128]{1,0:T(8,128)}) %reduce-scatter.5.cloned.1.call-update) | async-done | bytes 16400 | tf_op jit(solution)/shard_map/reduce_scatter | solution.py:90
  168.4 9.3 %all_gather.22 = f32[32,512]{1,0:T(8,128)S(1)} all-gather(f32[32,128]{1,0:T(8,128)} %reduce-scatter.5.cloned.1.call-done), channel_id=1, replica_groups=mesh['sub'=16,'row'=4,'col'=8] {'row'}, dimensions={1}, use_global_device_ids=true | all-gather | bytes 81920 | tf_op jit(solution)/shard_map/all_gather | solution.py:115
  177.7 1.7 convolution_select_fusion.3
  179.3 0.0 all-reduce.4.cloned.1.call-update
  179.4 0.0 all-gather.5.cloned.1.call-start
  179.4 2.0 convolution_select_fusion.1
  181.4 0.0 all-gather.5.cloned.1.call-update
  181.4 0.0 all-reduce.6.cloned.1.call-start
  181.5 123.4 %all-reduce.4.cloned.1.call-done = f32[32,512]{1,0:T(8,128)} async-done(((f32[32,512]{1,0:T(8,128)}), f32[32,512]{1,0:T(8,128)}) %all-reduce.4.cloned.1.call-update) | async-done | bytes 65552 | tf_op jit(solution)/shard_map/psum | solution.py:11
  304.9 1.3 fusion.3
  306.2 9.7 %all_gather.23 = f32[32,512]{1,0:T(8,128)S(1)} all-gather(f32[32,128]{1,0:T(8,128)S(1)} %fusion.3), channel_id=1, replica_groups=mesh['sub'=16,'row'=4,'col'=8] {'row'}, dimensions={1}, use_global_device_ids=true | all-gather | bytes 81920 | tf_op jit(solution)/shard_map/all_gather | solution.py:115
  316.0 1.7 convolution_select_fusion.2
  317.7 27.0 %all-gather.5.cloned.1.call-done = f32[512,512]{1,0:T(8,128)} async-done(((f32[128,512]{1,0:T(8,128)}), f32[512,512]{1,0:T(8,128)}) %all-gather.5.cloned.1.call-update) | async-done | bytes 1048592 | tf_op jit(solution)/shard_map/all_gather | solution.py:108
  344.7 1.1 broadcast_select_fusion
  345.8 0.0 all-reduce.6.cloned.1.call-update
  345.8 0.1 dynamic-slice_bitcast_fusion.1
  345.9 133.4 %all-reduce.6.cloned.1.call-done = (f32[512,512]{1,0:T(8,128)}, f32[32,512]{1,0:T(8,128)}) async-done(((f32[512,512]{1,0:T(8,128)}, f32[32,512]{1,0:T(8,128)}), (f32[512,512]{1,0:T(8,128)}, f32[32,512]{1,0:T(8,128)})) %all-reduce.6.cloned.1.call-update) | async-done | bytes 1114128 | tf_op jit(solution)/shard_map/psum | solution.py:11
  479.3 1.3 convolution_subtract_fusion.1
  480.6 23.2 %all_gather.21 = f32[512,128]{1,0:T(8,128)S(1)} all-gather(f32[64,128]{1,0:T(8,128)S(1)} %convolution_subtract_fusion.1), channel_id=1, replica_groups=mesh['sub'=16,'row'=4,'col'=8] {'col'}, dimensions={0}, use_global_device_ids=true | all-gather | bytes 294912 | tf_op jit(solution)/shard_map/all_gather | solution.py:100
  503.8 1.3 convolution_select_fusion
  505.1 0.1 dynamic-slice_bitcast_fusion
  505.2 0.7 copy.13
  505.9 1.0 fusion.2
  (26 shorter events, 0.1 us)
Async XLA Ops:
  7.2 46.8 %all-gather.3.cloned.1.call-start = ((), (), s32[]{:S(2)}) async-start(), calls=%async_computation.2 | async-start | bytes 2621440 | tf_op jit(solution)/shard_map/all_gather | solution.py:50
  9.8 47.0 %copy-start.2 = (f32[256,512]{1,0:T(8,128)S(1)}, f32[256,512]{1,0:T(8,128)}, u32[]{:S(2)}) copy-start(f32[256,512]{1,0:T(8,128)} %bitcast_select_fusion) | copy-start | bytes 1572868
  9.8 111.4 %reduce-scatter.3.cloned.1.call-start = ((), (), s32[]{:S(2)}) async-start(), calls=%async_computation.3 | async-start | bytes 1114112 | tf_op jit(solution)/shard_map/reduce_scatter | solution.py:61
  56.8 3.8 copy-start.5
  56.8 3.8 copy-start.7
  57.8 64.3 %copy-start.6 = (s32[256]{0:T(256)S(1)}, s32[256]{0:T(256)}, u32[]{:S(2)}) copy-start(s32[256]{0:T(256)} %param.14) | copy-start | bytes 3076
  57.9 119.8 %copy-start = (f32[2,512,512]{2,1,0:T(8,128)S(1)}, f32[2,512,512]{2,1,0:T(8,128)}, u32[]{:S(2)}) copy-start(f32[2,512,512]{2,1,0:T(8,128)} %param.15) | copy-start | bytes 6291460
  60.5 107.8 %reduce-scatter.5.cloned.1.call-start = ((), (), s32[]{:S(2)}) async-start(), calls=%async_computation.5 | async-start | bytes 147456 | tf_op jit(solution)/shard_map/reduce_scatter | solution.py:90
  123.1 181.8 %all-reduce.4.cloned.1.call-start = ((), (), s32[]{:S(2)}) async-start(), calls=%async_computation.6 | async-start | bytes 131072 | tf_op jit(solution)/shard_map/psum | solution.py:11
  168.4 136.6 %copy-start.3 = (f32[32,128]{1,0:T(8,128)S(1)}, f32[32,128]{1,0:T(8,128)}, u32[]{:S(2)}) copy-start(f32[32,128]{1,0:T(8,128)} %reduce-scatter.5.cloned.1.call-done) | copy-start | bytes 49156
  179.4 165.3 %all-gather.5.cloned.1.call-start = ((), (), s32[]{:S(2)}) async-start(), calls=%async_computation.4 | async-start | bytes 1310720 | tf_op jit(solution)/shard_map/all_gather | solution.py:108
  181.4 297.9 %all-reduce.6.cloned.1.call-start = ((), (), s32[]{:S(2)}) async-start(), calls=%async_computation.7 | async-start | bytes 2228224 | tf_op jit(solution)/shard_map/psum | solution.py:11
  316.0 29.8 %copy-start.1 = (f32[128,512]{1,0:T(8,128)S(1)}, f32[128,512]{1,0:T(8,128)}, u32[]{:S(2)}) copy-start(f32[128,512]{1,0:T(8,128)} %convolution_select_fusion.1) | copy-start | bytes 786436
  479.3 26.6 %copy-start.4 = (f32[32,512]{1,0:T(8,128)S(1)}, f32[32,512]{1,0:T(8,128)}, u32[]{:S(2)}) copy-start(f32[32,512]{1,0:T(8,128)} %get-tuple-element.10) | copy-start | bytes 196612
Sparse Core Ops, SparseCore 0:
  10.1 43.8 all-gather.2
  60.7 60.4 reduce-scatter.2
  124.2 44.0 reduce-scatter.4
  179.5 125.3 all-reduce.3
  307.1 37.5 all-gather.4
  347.7 131.5 all-reduce.5
where the time goes:
time: 514 us
  waiting for transfers between devices  407 us (79%)
  blocking collectives  65.8 us (13%)
  matrix products  17.6 us (3%)
  between operations  15 us (3%)
    psum x2, waiting for transfers between devices, from_root(): return lax.psum(jnp.where(mine, value, jnp.zeros_like(value)), axis)  257 us
    reduce_scatter x1, waiting for transfers between devices, on_device(): lax.psum_scatter(contribution, 'sub', scatter_dimension=1, tiled=True)  58 us
    all_gather x2, blocking collectives, on_device(): lax.all_gather(column_slabs[panel_index], 'col', axis=0, tiled=True)  46.8 us
    all_gather x1, waiting for transfers between devices, on_device(): lax.all_gather(live_factor, 'row', axis=1, tiled=True)  43.3 us
    all_gather x1, waiting for transfers between devices, on_device(): lax.all_gather(panel_now, 'row', axis=0, tiled=True)  27 us
    reduce_scatter x1, waiting for transfers between devices, on_device(): lax.psum_scatter(jnp.dot(chooser, front_cols, precision=PRECISE), 'col',...  21.6 us
    all_gather x2, blocking collectives, on_device(): gathered = lax.all_gather(right_side, 'row', axis=1, tiled=True)  19 us
    dot_general x9, matrix products, contract(): lax.dot_general(left_part, right_part, (((left_dim,), (right_dim,)), ((),...  13.9 us
  transfers between devices with their start and end apart: 6, of which 6 were waited for; matrix products, arithmetic and copies ran while one was open for 2% of the time, Pallas kernels for 0%

commit v1 on v0

--- a/solution.py
+++ b/solution.py
@@ -8,7 +8,7 @@
 
 def from_root(value, axis, root):
     mine = lax.axis_index(axis) == root
-    return lax.psum(jnp.where(mine, value, jnp.zeros_like(value)), axis)
+    return jnp.sum(lax.all_gather(jnp.where(mine, value, jnp.zeros_like(value)), axis), axis=0)
 
 
 def contract(left_part, right_part, left_dim, right_dim):

time: 514 us -> 580 us (1.13)
  waiting for transfers between devices: 407 us -> 475 us
  blocking collectives: 65.8 us -> 50.7 us
  other arithmetic: 4.24 us -> 16.4 us
    all_gather x0 -> x3, waiting for transfers between devices: none -> 304 us  [from_root(): lax.all_gather(jnp.where(mine, value, jnp.zeros_like(value)), axis)]
    psum x2 -> x0, waiting for transfers between devices: 257 us -> none  [from_root(): return lax.psum(jnp.where(mine, value, jnp.zeros_like(value)), axis)]
    reduce_scatter x1, waiting for transfers between devices: 21.6 us -> 45.3 us  [on_device(): lax.psum_scatter(jnp.dot(chooser, front_cols, precision=PRECISE), 'col',...]
    all_gather x2, blocking collectives: 46.8 us -> 31.7 us  [on_device(): lax.all_gather(column_slabs[panel_index], 'col', axis=0, tiled=True)]
    reduce_sum x0 -> x3, other arithmetic: none -> 10.5 us  [from_root(): jnp.sum(lax.all_gather(jnp.where(mine, value, jnp.zeros_like(value)), axi...]
  transfers between devices with their start and end apart: 6 -> 7, of which waited for: 6 -> 7; matrix products, arithmetic and copies ran while one was open for 2% -> 2% of each run, Pallas kernels for 0% -> 0%
where the time goes in v1:
time: 580 us; the launch traced here: 579 us
  waiting for transfers between devices  475 us (82%)
  blocking collectives  50.7 us (9%)
  matrix products  17.4 us (3%)
  other arithmetic  16.4 us (3%)
  between operations  15 us (3%)
    all_gather x3, waiting for transfers between devices, from_root(): lax.all_gather(jnp.where(mine, value, jnp.zeros_like(value)), axis)  304 us
    reduce_scatter x1, waiting for transfers between devices, on_device(): lax.psum_scatter(contribution, 'sub', scatter_dimension=1, tiled=True)  56.8 us
    reduce_scatter x1, waiting for transfers between devices, on_device(): lax.psum_scatter(jnp.dot(chooser, front_cols, precision=PRECISE), 'col',...  45.3 us
    all_gather x1, waiting for transfers between devices, on_device(): lax.all_gather(live_factor, 'row', axis=1, tiled=True)  43.3 us
    all_gather x2, blocking collectives, on_device(): lax.all_gather(column_slabs[panel_index], 'col', axis=0, tiled=True)  31.7 us
    all_gather x1, waiting for transfers between devices, on_device(): lax.all_gather(panel_now, 'row', axis=0, tiled=True)  24.9 us
    all_gather x2, blocking collectives, on_device(): gathered = lax.all_gather(right_side, 'row', axis=1, tiled=True)  19 us
    dot_general x9, matrix products, contract(): lax.dot_general(left_part, right_part, (((left_dim,), (right_dim,)), ((),...  13.6 us
  transfers between devices with their start and end apart: 7, of which 7 were waited for; matrix products, arithmetic and copies ran while one was open for 2% of the time, Pallas kernels for 0%

profile of v1, /device:TPU:1, one launch (start us, length us, event | category | flops | bytes accessed | tf_op | source)
XLA Modules:
  0.0 579.3 jit_solution(5218810932421864921)
XLA Ops:
  7.2 0.0 all-gather.9.cloned.1.call-start
  7.9 1.9 bitcast_select_fusion
  9.8 0.0 all-gather.9.cloned.1.call-update
  9.8 0.0 reduce-scatter.3.cloned.1.call-start
  9.9 0.1 iota_add_fusion
  9.9 0.1 add.286
  10.0 0.7 constant_dynamic-slice_fusion
  10.7 43.3 %all-gather.9.cloned.1.call-done = f32[256,2048]{1,0:T(8,128)} async-done(((f32[256,512]{1,0:T(8,128)}), f32[256,2048]{1,0:T(8,128)}) %all-gather.9.cloned.1.call-update) | async-done | bytes 2097168 | tf_op jit(solution)/shard_map/all_gather | solution.py:50
  54.0 2.8 fusion.8
  56.8 1.0 convolution_subtract_fusion
  57.9 2.7 fusion
  60.5 0.0 reduce-scatter.5.cloned.1.call-start
  60.6 0.5 broadcast_compare_fusion.3
  61.1 0.6 broadcast_add_fusion.1
  61.7 0.1 select_reduce_fusion
  61.9 1.1 gather_fusion
  63.1 1.1 gather_fusion.1
  64.3 56.8 %reduce-scatter.3.cloned.1.call-done = f32[128,128]{1,0:T(8,128)} async-done(((f32[128,2048]{1,0:T(8,128)}), f32[128,128]{1,0:T(8,128)}) %reduce-scatter.3.cloned.1.call-update) | async-done | bytes 65552 | tf_op jit(solution)/shard_map/reduce_scatter | solution.py:61
  121.0 0.9 select_add_fusion
  122.0 0.9 fusion.17
  122.9 0.0 all-gather.15.cloned.1.call-start
  123.0 45.3 %reduce-scatter.5.cloned.1.call-done = f32[32,128]{1,0:T(8,128)} async-done(((f32[256,128]{1,0:T(8,128)}), f32[32,128]{1,0:T(8,128)}) %reduce-scatter.5.cloned.1.call-update) | async-done | bytes 16400 | tf_op jit(solution)/shard_map/reduce_scatter | solution.py:90
  168.3 9.2 %all_gather.42 = f32[32,512]{1,0:T(8,128)S(1)} all-gather(f32[32,128]{1,0:T(8,128)} %reduce-scatter.5.cloned.1.call-done), channel_id=1, replica_groups=mesh['sub'=16,'row'=4,'col'=8] {'row'}, dimensions={1}, use_global_device_ids=true | all-gather | bytes 81920 | tf_op jit(solution)/shard_map/all_gather | solution.py:115
  177.5 1.7 convolution_select_fusion.3
  179.2 0.0 all-gather.11.cloned.1.call-start
  179.2 18.1 %all_gather.37 = f32[512,128]{1,0:T(8,128)S(1)} all-gather(f32[64,128]{1,0:T(8,128)S(1)} %unstack.10), channel_id=1, replica_groups=mesh['sub'=16,'row'=4,'col'=8] {'col'}, dimensions={0}, use_global_device_ids=true | all-gather | bytes 294912 | tf_op jit(solution)/shard_map/all_gather | solution.py:100
  197.3 2.0 convolution_select_fusion.1
  199.4 0.0 all-gather.17.cloned.1.call-start
  199.4 0.6 broadcast_compare_fusion.2
  200.0 43.9 %all-gather.15.cloned.1.call-done = f32[512,512]{1,0:T(8,128)} async-done(((f32[32,512]{1,0:T(8,128)}), f32[512,512]{1,0:T(8,128)}) %all-gather.15.cloned.1.call-update) | async-done | bytes 1048592 | tf_op jit(solution)/shard_map/all_gather | solution.py:11
  243.9 1.3 reduce_sum.38
  245.2 1.3 fusion.3
  246.6 9.8 %all_gather.45 = f32[32,512]{1,0:T(8,128)S(1)} all-gather(f32[32,128]{1,0:T(8,128)S(1)} %fusion.3), channel_id=1, replica_groups=mesh['sub'=16,'row'=4,'col'=8] {'row'}, dimensions={1}, use_global_device_ids=true | all-gather | bytes 81920 | tf_op jit(solution)/shard_map/all_gather | solution.py:115
  256.3 1.7 convolution_select_fusion.2
  258.0 0.2 all-gather.13.cloned.1.call-start
  258.3 24.9 %all-gather.11.cloned.1.call-done = f32[512,512]{1,0:T(8,128)} async-done(((f32[128,512]{1,0:T(8,128)}), f32[512,512]{1,0:T(8,128)}) %all-gather.11.cloned.1.call-update) | async-done | bytes 1048592 | tf_op jit(solution)/shard_map/all_gather | solution.py:108
  283.1 1.1 broadcast_select_fusion
  284.3 0.7 dynamic-slice_bitcast_fusion.1
  285.0 63.0 %all-gather.17.cloned.1.call-done = f32[512,512]{1,0:T(8,128)} async-done(((f32[32,512]{1,0:T(8,128)}), f32[512,512]{1,0:T(8,128)}) %all-gather.17.cloned.1.call-update) | async-done | bytes 1048592 | tf_op jit(solution)/shard_map/all_gather | solution.py:11
  348.0 1.3 reduce_sum.39
  349.3 197.4 %all-gather.13.cloned.1.call-done = f32[8192,512]{1,0:T(8,128)} async-done(((f32[512,512]{1,0:T(8,128)}), f32[8192,512]{1,0:T(8,128)}) %all-gather.13.cloned.1.call-update) | async-done | bytes 16777232 | tf_op jit(solution)/shard_map/all_gather | solution.py:11
  546.6 7.9 %reduce_sum.37 = f32[512,512]{1,0:T(8,128)S(1)} reduce(f32[16,512,512]{2,1,0:T(8,128)} %bitcast.46, f32[]{:T(128)} %constant.128.clone.1), dimensions={0}, to_apply=%region_2.4 | reduce | flops 3932160 | bytes 17825796 | tf_op jit(solution)/shard_map/reduce_sum | solution.py:11
  554.6 0.4 convolution_subtract_fusion.1
  555.0 13.7 %all_gather.41 = f32[512,128]{1,0:T(8,128)S(1)} all-gather(f32[64,128]{1,0:T(8,128)S(1)} %convolution_subtract_fusion.1), channel_id=1, replica_groups=mesh['sub'=16,'row'=4,'col'=8] {'col'}, dimensions={0}, use_global_device_ids=true | all-gather | bytes 294912 | tf_op jit(solution)/shard_map/all_gather | solution.py:100
  568.6 2.0 convolution_select_fusion
  570.6 0.1 dynamic-slice_bitcast_fusion
  570.7 0.7 copy.13
  571.4 1.0 fusion.2
  (36 shorter events, 0.2 us)
Async XLA Ops:
  7.2 46.8 %all-gather.9.cloned.1.call-start = ((), (), s32[]{:S(2)}) async-start(), calls=%async_computation.2 | async-start | bytes 2621440 | tf_op jit(solution)/shard_map/all_gather | solution.py:50
  9.8 47.0 %copy-start.2 = (f32[256,512]{1,0:T(8,128)S(1)}, f32[256,512]{1,0:T(8,128)}, u32[]{:S(2)}) copy-start(f32[256,512]{1,0:T(8,128)} %bitcast_select_fusion) | copy-start | bytes 1572868
  9.8 111.2 %reduce-scatter.3.cloned.1.call-start = ((), (), s32[]{:S(2)}) async-start(), calls=%async_computation.3 | async-start | bytes 1114112 | tf_op jit(solution)/shard_map/reduce_scatter | solution.py:61
  56.8 4.9 copy-start.5
  56.8 4.9 copy-start.9
  57.8 64.1 %copy-start.8 = (s32[256]{0:T(256)S(1)}, s32[256]{0:T(256)}, u32[]{:S(2)}) copy-start(s32[256]{0:T(256)} %param.14) | copy-start | bytes 3076
  57.9 119.6 %copy-start = (f32[2,512,512]{2,1,0:T(8,128)S(1)}, f32[2,512,512]{2,1,0:T(8,128)}, u32[]{:S(2)}) copy-start(f32[2,512,512]{2,1,0:T(8,128)} %param.15) | copy-start | bytes 6291460
  60.5 107.8 %reduce-scatter.5.cloned.1.call-start = ((), (), s32[]{:S(2)}) async-start(), calls=%async_computation.5 | async-start | bytes 147456 | tf_op jit(solution)/shard_map/reduce_scatter | solution.py:90
  122.9 121.0 %all-gather.15.cloned.1.call-start = ((), (), s32[]{:S(2)}) async-start(), calls=%async_computation.7 | async-start | bytes 1114112 | tf_op jit(solution)/shard_map/all_gather | solution.py:11
  177.5 67.7 %copy-start.4 = (f32[32,128]{1,0:T(8,128)S(1)}, f32[32,128]{1,0:T(8,128)}, u32[]{:S(2)}) copy-start(f32[32,128]{1,0:T(8,128)} %reduce-scatter.5.cloned.1.call-done) | copy-start | bytes 49156
  179.2 104.0 %all-gather.11.cloned.1.call-start = ((), (), s32[]{:S(2)}) async-start(), calls=%async_computation.4 | async-start | bytes 1310720 | tf_op jit(solution)/shard_map/all_gather | solution.py:108
  199.4 148.6 %all-gather.17.cloned.1.call-start = ((), (), s32[]{:S(2)}) async-start(), calls=%async_computation.8 | async-start | bytes 1114112 | tf_op jit(solution)/shard_map/all_gather | solution.py:11
  256.3 27.9 %copy-start.1 = (f32[128,512]{1,0:T(8,128)S(1)}, f32[128,512]{1,0:T(8,128)}, u32[]{:S(2)}) copy-start(f32[128,512]{1,0:T(8,128)} %convolution_select_fusion.1) | copy-start | bytes 786436
  258.0 288.6 %all-gather.13.cloned.1.call-start = ((), (), s32[]{:S(2)}) async-start(), calls=%async_computation.6 | async-start | bytes 17825792 | tf_op jit(solution)/shard_map/all_gather | solution.py:11
  554.5 16.1 %copy-start.3 = (f32[1,64,128]{1,2,0:T(8,128)S(1)}, f32[1,64,128]{1,2,0:T(8,128)}, u32[]{:S(2)}) copy-start(f32[1,64,128]{1,2,0:T(8,128)} %dynamic-slice_bitcast_fusion.1) | copy-start | bytes 98308
  555.0 16.5 %copy-start.6 = (pred[128]{0:T(512)(128)(4,1)S(1)}, pred[128]{0:T(512)(128)(4,1)}, u32[]{:S(2)}) copy-start(pred[128]{0:T(512)(128)(4,1)} %get-tuple-element.9) | copy-start | bytes 388
  555.0 16.5 %copy-start.7 = (pred[128]{0:T(512)(128)(4,1)S(1)}, pred[128]{0:T(512)(128)(4,1)}, u32[]{:S(2)}) copy-start(pred[128]{0:T(512)(128)(4,1)} %get-tuple-element.14) | copy-start | bytes 388
Sparse Core Ops, SparseCore 0:
  10.1 43.8 all-gather.8
  60.7 60.3 reduce-scatter.2
  124.0 44.2 reduce-scatter.4
  179.3 64.5 all-gather.14
  245.9 37.2 all-gather.10
  285.1 62.8 all-gather.16
  350.0 196.5 all-gather.12
